TPU v7x, 128 devices: a whole 4x4x4 slice. The times are simulated.
128 devices in a mesh: row: 8 (over x, core), col: 16 (over z, y).
Axes of the slice: x: 4, y: 4, z: 4, core: 2. Of those that a mesh axis runs over, the one named last changes fastest.
Arguments:
- features: float32 [32768, 128], P('col', 'row'), may hold values from -6 to 6
- tile_rows: int32 [8, 16, 80], P('row', 'col'), may hold values from 0 to 32, as said below
- tile_cols: int32 [8, 16, 80], P('row', 'col'), may hold values from 0 to 15
- tile_values: float32 [8, 16, 80, 128, 128], P('row', 'col'), may hold values from -0.51881118 to 0.51881118, as said below
- weight_in: float32 [128, 256], replicated, may hold values from -0.5 to 0.5
- weight_out: float32 [256, 256], replicated, may hold values from -0.375 to 0.375
- cotangent: float32 [32768, 256], P(('col', 'row')), may hold values from -0.03125 to 0.03125
Outputs:
- output: float32 [32768, 256], P(('col', 'row'))
- grad_in: float32 [128, 256], replicated
- grad_out: float32 [256, 256], replicated
Inputs may be any that keep to these rules, and one draw needn't show every extreme that they name: `tile_rows`: slot s of device (i, j) is used for s below that device's tile count and holds a tile row 0 to 31; unused slots hold 32. Used slots come first, no (row, column) pair repeats within a device, and in every draw some device uses all 80 slots. `tile_values`: A tile is sparse: each entry is nonzero with probability 2.56 / 128, at random positions.
All inputs are finite; a program needn't handle non-finite values.
Results may differ from a plain program's by a relative error of at most 0.0003.
Values sent between devices are 32-bit elements; how exact they have to be, the bound alone decides.
A program may use at most 128 MiB of HBM per device.

v0:
```python
import jax
import jax.numpy as jnp
from jax import lax
from jax.sharding import PartitionSpec as P

TILE = 128


def forward_tiles(gathered, tile_row, tile_col, tile_block, out_tiles):
    width = gathered.shape[1]
    blocks = gathered.reshape(-1, TILE, width)
    picked = jnp.take(blocks, tile_col, axis=0)
    products = jnp.einsum("tab,tbf->taf", tile_block, picked, precision=lax.Precision.HIGHEST)
    onehot = (tile_row[None, :] == jnp.arange(out_tiles, dtype=jnp.int32)[:, None]).astype(
        jnp.float32
    )
    summed = jnp.einsum("rt,taf->raf", onehot, products, precision=lax.Precision.HIGHEST)
    return summed.reshape(out_tiles * TILE, width)


def adjoint_tiles(row_grads, tile_row, tile_col, tile_block, out_tiles):
    width = row_grads.shape[1]
    in_tiles = row_grads.shape[0] // TILE
    blocks = row_grads.reshape(in_tiles, TILE, width)
    picked = jnp.take(blocks, jnp.minimum(tile_row, in_tiles - 1), axis=0)
    products = jnp.einsum("tba,tbf->taf", tile_block, picked, precision=lax.Precision.HIGHEST)
    matches = tile_col[None, :] == jnp.arange(out_tiles, dtype=jnp.int32)[:, None]
    onehot = (matches & (tile_row < in_tiles)[None, :]).astype(jnp.float32)
    summed = jnp.einsum("rt,taf->raf", onehot, products, precision=lax.Precision.HIGHEST)
    return summed.reshape(out_tiles * TILE, width)


def dense_product(left, right):
    return jnp.dot(left, right, precision=lax.Precision.HIGHEST, preferred_element_type=jnp.float32)


def inner_rows(left, right):
    return lax.dot_general(
        left,
        right,
        (((0,), (0,)), ((), ())),
        precision=lax.Precision.HIGHEST,
        preferred_element_type=jnp.float32,
    )


def per_device(features, tile_rows, tile_cols, tile_values, weight_in, weight_out, cotangent):
    tile_row = tile_rows.reshape(-1)
    tile_col = tile_cols.reshape(-1)
    tile_block = tile_values.reshape(-1, TILE, TILE)
    local_rows = cotangent.shape[0]
    row_tiles = lax.axis_size("col") * local_rows // TILE
    col_tiles = lax.axis_size("row") * local_rows // TILE
    x_local = lax.all_to_all(features, "row", split_axis=0, concat_axis=1, tiled=True)
    support = dense_product(x_local, weight_in)
    gathered = lax.all_gather(support, "row", axis=0, tiled=True)
    partial_one = forward_tiles(gathered, tile_row, tile_col, tile_block, row_tiles)
    pre_act = lax.psum_scatter(partial_one, "col", scatter_dimension=0, tiled=True)
    hidden = jax.nn.silu(pre_act)
    support_two = dense_product(hidden, weight_out)
    gathered_two = lax.all_gather(support_two, "row", axis=0, tiled=True)
    partial_two = forward_tiles(gathered_two, tile_row, tile_col, tile_block, row_tiles)
    output = lax.psum_scatter(partial_two, "col", scatter_dimension=0, tiled=True)
    rows_out = lax.all_gather(cotangent, "col", axis=0, tiled=True)
    adjoint_two = adjoint_tiles(rows_out, tile_row, tile_col, tile_block, col_tiles)
    d_support_two = lax.psum_scatter(adjoint_two, "row", scatter_dimension=0, tiled=True)
    grad_out_local = inner_rows(hidden, d_support_two)
    d_hidden = dense_product(d_support_two, weight_out.T)
    sigmoid_pre = jax.nn.sigmoid(pre_act)
    d_pre = d_hidden * sigmoid_pre * (1.0 + pre_act * (1.0 - sigmoid_pre))
    rows_in = lax.all_gather(d_pre, "col", axis=0, tiled=True)
    adjoint_one = adjoint_tiles(rows_in, tile_row, tile_col, tile_block, col_tiles)
    d_support = lax.psum_scatter(adjoint_one, "row", scatter_dimension=0, tiled=True)
    grad_in_local = inner_rows(x_local, d_support)
    grad_in, grad_out = lax.psum((grad_in_local, grad_out_local), ("row", "col"))
    return (output, grad_in, grad_out)


def solution(mesh):
    return jax.shard_map(
        per_device,
        mesh=mesh,
        in_specs=(
            P("col", "row"),
            P("row", "col", None),
            P("row", "col", None),
            P("row", "col", None, None, None),
            P(),
            P(),
            P(("col", "row"), None),
        ),
        out_specs=(P(("col", "row"), None), P(), P()),
        check_vma=False,
    )
```

profile of v0, /device:TPU:0, one launch (start us, length us, event | category | flops | bytes accessed | tf_op | source)
XLA Modules:
  0.0 643.5 jit_solution(13298213714380566996)
XLA Ops:
  8.9 10.3 %all_to_all.19 = f32[8,256,16]{1,2,0:T(8,128)S(1)} all-to-all(f32[8,256,16]{1,2,0:T(8,128)S(1)} %bitcast.80), channel_id=1, replica_groups=mesh['row'=8,'col'=16] {'row'}, dimensions={0} | all-to-all | bytes 262144 | tf_op jit(solution)/shard_map/all_to_all | solution.py:54
  22.0 42.2 %all-gather.9.cloned.1.call-done = f32[4096,256]{1,0:T(8,128)} async-done(((f32[256,256]{1,0:T(8,128)}), f32[4096,256]{1,0:T(8,128)}) %all-gather.9.cloned.1.call-update) | async-done | bytes 4194320 | tf_op jit(solution)/shard_map/all_gather | solution.py:64
  64.2 9.9 %gather_fusion.2 = f32[80,128,256]{2,1,0:T(8,128)} fusion(f32[32,128,256]{2,1,0:T(8,128)} %bitcast.72, s32[1024]{0:T(1024)S(1)} %pad_clamp_fusion), kind=kCustom, calls=%fused_computation.1.clone | custom fusion | bytes 20971840 | tf_op jit(solution)/shard_map/jit(_take)/gather | solution.py:25
  74.0 23.1 %fusion.30 = f32[80,128,256]{1,2,0:T(8,128)} fusion(f32[1,1,80,128,128]{4,3,2,1,0:T(8,128)} %param.14, f32[80,128,256]{2,1,0:T(8,128)} %gather_fusion.2, pred[80]{0:T(512)(128)(4,1)S(1)} %get-tuple-element.22), kind=kOutput, calls=%fused_computation.26 | convolution fusion | flops 4029153280 | bytes 26214480 | tf_op jit(solution)/shard_map/tba,tbf->taf/dot_general | solution.py:26
  97.2 11.6 %copy.48 = f32[80,128,256]{2,0,1:T(8,128)} copy(f32[80,128,256]{1,2,0:T(8,128)} %fusion.30) | data formatting | bytes 20971520 | tf_op jit(solution)/shard_map/tba,tbf->taf/dot_general | solution.py:26
  108.8 6.2 fusion.57
  118.1 9.9 %gather_fusion = f32[80,128,256]{2,1,0:T(8,128)} fusion(f32[16,128,256]{2,1,0:T(8,128)} %bitcast.70, s32[1024]{0:T(1024)S(1)} %pad_clamp_fusion.1), kind=kCustom, calls=%fused_computation.clone | custom fusion | bytes 20971840 | tf_op jit(solution)/shard_map/jit(_take)/gather | solution.py:12
  128.0 23.0 %fusion.20 = f32[80,128,256]{1,2,0:T(8,128)} fusion(f32[1,1,80,128,128]{4,3,2,1,0:T(8,128)} %param.14, f32[80,128,256]{2,1,0:T(8,128)} %gather_fusion, pred[80]{0:T(512)(128)(4,1)S(1)} %compare_and_fusion.1), kind=kOutput, calls=%fused_computation.24 | convolution fusion | flops 4029153280 | bytes 26214480 | tf_op jit(solution)/shard_map/tab,tbf->taf/dot_general | solution.py:13
  151.0 11.7 %copy.42 = f32[80,128,256]{2,0,1:T(8,128)} copy(f32[80,128,256]{1,2,0:T(8,128)} %fusion.20) | data formatting | bytes 20971520 | tf_op jit(solution)/shard_map/tab,tbf->taf/dot_general | solution.py:13
  162.7 6.9 %fusion.49 = f32[32,128,256]{2,0,1:T(8,128)S(1)} fusion(f32[80,128,256]{2,0,1:T(8,128)} %copy.42, s32[80]{0:T(128)S(1)} %bitcast.82), kind=kOutput, calls=%fused_computation.39 | convolution fusion | flops 1006635520 | bytes 14680384 | tf_op jit(solution)/shard_map/rt,taf->raf/dot_general | solution.py:17
  169.6 4.4 copy.43
  174.0 78.6 %reduce-scatter.5.cloned.1.call-done = f32[256,256]{1,0:T(8,128)} async-done(((f32[4096,256]{1,0:T(8,128)}), f32[256,256]{1,0:T(8,128)}) %reduce-scatter.5.cloned.1.call-update) | async-done | bytes 262160 | tf_op jit(solution)/shard_map/reduce_scatter | solution.py:58
  257.0 48.8 %all-gather.11.cloned.1.call-done = f32[4096,256]{1,0:T(8,128)} async-done(((f32[256,256]{1,0:T(8,128)}), f32[4096,256]{1,0:T(8,128)}) %all-gather.11.cloned.1.call-update) | async-done | bytes 4194320 | tf_op jit(solution)/shard_map/all_gather | solution.py:71
  305.8 10.1 %gather_fusion.3 = f32[80,128,256]{2,1,0:T(8,128)} fusion(f32[32,128,256]{2,1,0:T(8,128)} %bitcast.73, s32[1024]{0:T(1024)S(1)} %pad_clamp_fusion), kind=kCustom, calls=%fused_computation.3.clone | custom fusion | bytes 20971840 | tf_op jit(solution)/shard_map/jit(_take)/gather | solution.py:25
  315.8 23.2 %fusion.35 = f32[80,128,256]{1,2,0:T(8,128)} fusion(f32[1,1,80,128,128]{4,3,2,1,0:T(8,128)} %param.14, f32[80,128,256]{2,1,0:T(8,128)} %gather_fusion.3, pred[80]{0:T(512)(128)(4,1)S(1)} %get-tuple-element.22), kind=kOutput, calls=%fused_computation.27 | convolution fusion | flops 4029153280 | bytes 26214480 | tf_op jit(solution)/shard_map/tba,tbf->taf/dot_general | solution.py:26
  339.1 11.6 %copy.51 = f32[80,128,256]{2,0,1:T(8,128)} copy(f32[80,128,256]{1,2,0:T(8,128)} %fusion.35) | data formatting | bytes 20971520 | tf_op jit(solution)/shard_map/tba,tbf->taf/dot_general | solution.py:26
  350.7 6.3 fusion.55
  361.2 9.8 %gather_fusion.1 = f32[80,128,256]{2,1,0:T(8,128)} fusion(f32[16,128,256]{2,1,0:T(8,128)} %bitcast.71, s32[1024]{0:T(1024)S(1)} %pad_clamp_fusion.1), kind=kCustom, calls=%fused_computation.2.clone | custom fusion | bytes 20971840 | tf_op jit(solution)/shard_map/jit(_take)/gather | solution.py:12
  371.0 23.0 %fusion.25 = f32[80,128,256]{1,2,0:T(8,128)} fusion(f32[1,1,80,128,128]{4,3,2,1,0:T(8,128)} %param.14, f32[80,128,256]{2,1,0:T(8,128)} %gather_fusion.1, pred[80]{0:T(512)(128)(4,1)S(1)} %compare_and_fusion.1), kind=kOutput, calls=%fused_computation.25 | convolution fusion | flops 4029153280 | bytes 26214480 | tf_op jit(solution)/shard_map/tab,tbf->taf/dot_general | solution.py:13
  394.0 11.6 %copy.45 = f32[80,128,256]{2,0,1:T(8,128)} copy(f32[80,128,256]{1,2,0:T(8,128)} %fusion.25) | data formatting | bytes 20971520 | tf_op jit(solution)/shard_map/tab,tbf->taf/dot_general | solution.py:13
  408.2 6.9 %fusion.47 = f32[32,128,256]{2,0,1:T(8,128)S(1)} fusion(f32[80,128,256]{2,0,1:T(8,128)} %copy.45, s32[80]{0:T(128)S(1)} %bitcast.83), kind=kOutput, calls=%fused_computation.38 | convolution fusion | flops 1006635520 | bytes 14680384 | tf_op jit(solution)/shard_map/rt,taf->raf/dot_general | solution.py:17
  415.1 4.4 copy.46
  419.4 134.7 %all-reduce.3.cloned.1.call-done = (f32[128,256]{0,1:T(8,128)}, f32[256,256]{1,0:T(8,128)}) async-done(((f32[128,256]{0,1:T(8,128)}, f32[256,256]{1,0:T(8,128)}), (f32[128,256]{0,1:T(8,128)}, f32[256,256]{1,0:T(8,128)})) %all-reduce.3.cloned.1.call-update) | async-done | bytes 393232 | tf_op jit(solution)/shard_map/psum | solution.py:75
  555.8 79.0 %reduce-scatter.7.cloned.1.call-done = f32[256,256]{1,0:T(8,128)} async-done(((f32[4096,256]{1,0:T(8,128)}), f32[256,256]{1,0:T(8,128)}) %reduce-scatter.7.cloned.1.call-update) | async-done | bytes 262160 | tf_op jit(solution)/shard_map/reduce_scatter | solution.py:63
  (49 shorter events, 21.9 us)
Async XLA Ops:
  7.2 245.4 %copy-start = (f32[256,256]{1,0:T(8,128)S(1)}, f32[256,256]{1,0:T(8,128)}, u32[]{:S(2)}) copy-start(f32[256,256]{1,0:T(8,128)} %param.16) | copy-start | bytes 786436
  7.2 57.0 %all-gather.9.cloned.1.call-start = ((), (), s32[]{:S(2)}) async-start(), calls=%async_computation.9 | async-start | bytes 4456448 | tf_op jit(solution)/shard_map/all_gather | solution.py:64
  7.9 110.2 %all-gather.5.cloned.1.call-start = ((), (), s32[]{:S(2)}) async-start(), calls=%async_computation.5 | async-start | bytes 2359296 | tf_op jit(solution)/shard_map/all_gather | solution.py:56
  21.2 152.8 %reduce-scatter.9.cloned.1.call-start = ((), (), s32[]{:S(2)}) async-start(), calls=%async_computation.10 | async-start | bytes 2359296 | tf_op jit(solution)/shard_map/reduce_scatter | solution.py:66
  97.2 11.7 %copy-start.3 = (s32[1,1,80]{2,1,0:T(1,128)S(1)}, s32[1,1,80]{2,1,0:T(1,128)}, u32[]{:S(2)}) copy-start(s32[1,1,80]{2,1,0:T(1,128)} %param.13) | copy-start | bytes 964
  117.7 134.9 %reduce-scatter.5.cloned.1.call-start = ((), (), s32[]{:S(2)}) async-start(), calls=%async_computation.6 | async-start | bytes 4456448 | tf_op jit(solution)/shard_map/reduce_scatter | solution.py:58
  151.0 11.7 %copy-start.2 = (s32[1,1,80]{2,1,0:T(1,128)S(1)}, s32[1,1,80]{2,1,0:T(1,128)}, u32[]{:S(2)}) copy-start(s32[1,1,80]{2,1,0:T(1,128)} %param.12) | copy-start | bytes 964
  174.0 131.8 %all-gather.11.cloned.1.call-start = ((), (), s32[]{:S(2)}) async-start(), calls=%async_computation.11 | async-start | bytes 4456448 | tf_op jit(solution)/shard_map/all_gather | solution.py:71
  254.8 106.4 %all-gather.7.cloned.1.call-start = ((), (), s32[]{:S(2)}) async-start(), calls=%async_computation.7 | async-start | bytes 2359296 | tf_op jit(solution)/shard_map/all_gather | solution.py:61
  256.9 148.7 %reduce-scatter.11.cloned.1.call-start = ((), (), s32[]{:S(2)}) async-start(), calls=%async_computation.12 | async-start | bytes 2359296 | tf_op jit(solution)/shard_map/reduce_scatter | solution.py:73
  350.7 9.2 %copy-start.4 = (f32[256,256]{1,0:T(8,128)S(1)}, f32[256,256]{1,0:T(8,128)}, u32[]{:S(2)}) copy-start(f32[256,256]{1,0:T(8,128)} %reduce-scatter.9.cloned.1.call-done) | copy-start | bytes 786436
  350.7 9.2 %copy-start.5 = (f32[256,256]{1,0:T(8,128)S(1)}, f32[256,256]{1,0:T(8,128)}, u32[]{:S(2)}) copy-start(f32[256,256]{1,0:T(8,128)} %reduce-scatter.5.cloned.1.call-done) | copy-start | bytes 786436
  359.6 194.6 %all-reduce.3.cloned.1.call-start = ((), (), s32[]{:S(2)}) async-start(), calls=%async_computation.13 | async-start | bytes 786432 | tf_op jit(solution)/shard_map/psum | solution.py:75
  407.9 228.7 %copy-start.1 = (f32[256,256]{1,0:T(8,128)S(1)}, f32[256,256]{1,0:T(8,128)}, u32[]{:S(2)}) copy-start(f32[256,256]{1,0:T(8,128)} %param.16) | copy-start | bytes 786436
  407.9 227.0 %reduce-scatter.7.cloned.1.call-start = ((), (), s32[]{:S(2)}) async-start(), calls=%async_computation.8 | async-start | bytes 4456448 | tf_op jit(solution)/shard_map/reduce_scatter | solution.py:63
Sparse Core Ops, SparseCore 0:
  10.1 53.9 all-gather.8
  66.5 24.8 all-gather.4
  117.8 33.6 reduce-scatter.8
  174.1 78.4 reduce-scatter.4
  255.1 50.5 all-gather.10
  307.9 24.8 all-gather.6
  359.7 33.6 reduce-scatter.10
  408.0 146.1 all-reduce.2
  558.1 76.7 reduce-scatter.6
where the time goes:
time: 653 us; the launch traced here: 644 us
  waiting for transfers between devices  384 us (59%)
  matrix products  128 us (20%)
  local copies, waits for them, and re-layouts  104 us (16%)
  between operations  14.4 us (2%)
  blocking collectives  10.3 us (2%)
    psum x1, waiting for transfers between devices, per_device(): lax.psum((grad_in_local, grad_out_local), ('row', 'col'))  135 us
    reduce_scatter x1, waiting for transfers between devices, per_device(): lax.psum_scatter(partial_two, 'col', scatter_dimension=0, tiled=True)  79 us
    reduce_scatter x1, waiting for transfers between devices, per_device(): lax.psum_scatter(partial_one, 'col', scatter_dimension=0, tiled=True)  78.6 us
    all_gather x1, waiting for transfers between devices, per_device(): rows_in = lax.all_gather(d_pre, 'col', axis=0, tiled=True)  48.8 us
    dot_general x2, matrix products, adjoint_tiles(): jnp.einsum('tba,tbf->taf', tile_block, picked, precision=lax.Precision.HI...  46.4 us
    dot_general x2, matrix products, forward_tiles(): jnp.einsum('tab,tbf->taf', tile_block, picked, precision=lax.Precision.HI...  46 us
    all_gather x1, waiting for transfers between devices, per_device(): rows_out = lax.all_gather(cotangent, 'col', axis=0, tiled=True)  42.2 us
    dot_general x2, local copies, waits for them, and re-layouts, forward_tiles(): jnp.einsum('tab,tbf->taf', tile_block, picked, precision=lax.Precision.HI...  23.3 us
  transfers between devices with their start and end apart: 9, of which 5 were waited for; matrix products, arithmetic and copies ran while one was open for 35% of the time, Pallas kernels for 0%

commit v1 on v0

--- a/solution.py
+++ b/solution.py
@@ -1,9 +1,18 @@
+import functools
 import jax
 import jax.numpy as jnp
 from jax import lax
 from jax.sharding import PartitionSpec as P
 
 TILE = 128
+
+
+def _follow_area(packet, mesh_name, lane_axis):
+    value_now = lax.psum(packet, mesh_name)
+    return lax.psum(value_now, lane_axis)
+
+
+define_array = functools.partial(_follow_area, mesh_name="col", lane_axis="row")
 
 
 def forward_tiles(gathered, tile_row, tile_col, tile_block, out_tiles):
@@ -72,7 +81,7 @@
     adjoint_one = adjoint_tiles(rows_in, tile_row, tile_col, tile_block, col_tiles)
     d_support = lax.psum_scatter(adjoint_one, "row", scatter_dimension=0, tiled=True)
     grad_in_local = inner_rows(x_local, d_support)
-    grad_in, grad_out = lax.psum((grad_in_local, grad_out_local), ("row", "col"))
+    grad_in, grad_out = define_array((grad_in_local, grad_out_local))
     return (output, grad_in, grad_out)
 
 

time: 653 us -> 644 us (0.986)
  waiting for transfers between devices: 384 us -> 375 us
    psum x1 -> x2, waiting for transfers between devices: 135 us -> 101 us  [the longest x1 50.8 us: _follow_area(): return lax.psum(value_now, lane_axis)]
    reduce_scatter x1, waiting for transfers between devices: 0.01 us -> 22.5 us  [per_device(): lax.psum_scatter(adjoint_one, 'row', scatter_dimension=0, tiled=True)]
  transfers between devices with their start and end apart: 9 -> 10, of which waited for: 5 -> 7; matrix products, arithmetic and copies ran while one was open for 35% -> 36% of each run, Pallas kernels for 0% -> 0%
where the time goes in v1:
time: 644 us; the launch traced here: 634 us
  waiting for transfers between devices  375 us (58%)
  matrix products  129 us (20%)
  local copies, waits for them, and re-layouts  104 us (16%)
  between operations  14.7 us (2%)
  blocking collectives  10.3 us (2%)
    reduce_scatter x1, waiting for transfers between devices, per_device(): lax.psum_scatter(partial_two, 'col', scatter_dimension=0, tiled=True)  80.2 us
    reduce_scatter x1, waiting for transfers between devices, per_device(): lax.psum_scatter(partial_one, 'col', scatter_dimension=0, tiled=True)  78.6 us
    psum x1, waiting for transfers between devices, _follow_area(): return lax.psum(value_now, lane_axis)  50.8 us
    psum x1, waiting for transfers between devices, _follow_area(): value_now = lax.psum(packet, mesh_name)  50.7 us
    all_gather x1, waiting for transfers between devices, per_device(): rows_in = lax.all_gather(d_pre, 'col', axis=0, tiled=True)  48.8 us
    dot_general x2, matrix products, adjoint_tiles(): jnp.einsum('tba,tbf->taf', tile_block, picked, precision=lax.Precision.HI...  46.5 us
    dot_general x2, matrix products, forward_tiles(): jnp.einsum('tab,tbf->taf', tile_block, picked, precision=lax.Precision.HI...  46.1 us
    all_gather x1, waiting for transfers between devices, per_device(): rows_out = lax.all_gather(cotangent, 'col', axis=0, tiled=True)  42.2 us
  transfers between devices with their start and end apart: 10, of which 7 were waited for; matrix products, arithmetic and copies ran while one was open for 36% of the time, Pallas kernels for 0%

profile of v1, /device:TPU:0, one launch (start us, length us, event | category | flops | bytes accessed | tf_op | source)
XLA Modules:
  0.0 634.2 jit_solution(5591188312396909658)
XLA Ops:
  8.9 10.3 %all_to_all.19 = f32[8,256,16]{1,2,0:T(8,128)S(1)} all-to-all(f32[8,256,16]{1,2,0:T(8,128)S(1)} %bitcast.80), channel_id=1, replica_groups=mesh['row'=8,'col'=16] {'row'}, dimensions={0} | all-to-all | bytes 262144 | tf_op jit(solution)/shard_map/all_to_all | solution.py:63
  22.0 42.2 %all-gather.9.cloned.1.call-done = f32[4096,256]{1,0:T(8,128)} async-done(((f32[256,256]{1,0:T(8,128)}), f32[4096,256]{1,0:T(8,128)}) %all-gather.9.cloned.1.call-update) | async-done | bytes 4194320 | tf_op jit(solution)/shard_map/all_gather | solution.py:73
  64.2 9.8 %gather_fusion.2 = f32[80,128,256]{2,1,0:T(8,128)} fusion(f32[32,128,256]{2,1,0:T(8,128)} %bitcast.72, s32[1024]{0:T(1024)S(1)} %pad_clamp_fusion), kind=kCustom, calls=%fused_computation.1.clone | custom fusion | bytes 20971840 | tf_op jit(solution)/shard_map/jit(_take)/gather | solution.py:34
  73.9 23.2 %fusion.30 = f32[80,128,256]{1,2,0:T(8,128)} fusion(f32[1,1,80,128,128]{4,3,2,1,0:T(8,128)} %param.14, f32[80,128,256]{2,1,0:T(8,128)} %gather_fusion.2, pred[80]{0:T(512)(128)(4,1)S(1)} %get-tuple-element.24), kind=kOutput, calls=%fused_computation.26 | convolution fusion | flops 4029153280 | bytes 26214480 | tf_op jit(solution)/shard_map/tba,tbf->taf/dot_general | solution.py:35
  97.1 11.7 %copy.48 = f32[80,128,256]{2,0,1:T(8,128)} copy(f32[80,128,256]{1,2,0:T(8,128)} %fusion.30) | data formatting | bytes 20971520 | tf_op jit(solution)/shard_map/tba,tbf->taf/dot_general | solution.py:35
  108.8 6.2 fusion.57
  118.1 9.8 %gather_fusion = f32[80,128,256]{2,1,0:T(8,128)} fusion(f32[16,128,256]{2,1,0:T(8,128)} %bitcast.70, s32[1024]{0:T(1024)S(1)} %pad_clamp_fusion.1), kind=kCustom, calls=%fused_computation.clone | custom fusion | bytes 20971840 | tf_op jit(solution)/shard_map/jit(_take)/gather | solution.py:21
  127.8 23.1 %fusion.20 = f32[80,128,256]{1,2,0:T(8,128)} fusion(f32[1,1,80,128,128]{4,3,2,1,0:T(8,128)} %param.14, f32[80,128,256]{2,1,0:T(8,128)} %gather_fusion, pred[80]{0:T(512)(128)(4,1)S(1)} %compare_and_fusion.1), kind=kOutput, calls=%fused_computation.24 | convolution fusion | flops 4029153280 | bytes 26214480 | tf_op jit(solution)/shard_map/tab,tbf->taf/dot_general | solution.py:22
  150.9 11.6 %copy.42 = f32[80,128,256]{2,0,1:T(8,128)} copy(f32[80,128,256]{1,2,0:T(8,128)} %fusion.20) | data formatting | bytes 20971520 | tf_op jit(solution)/shard_map/tab,tbf->taf/dot_general | solution.py:22
  162.6 6.9 %fusion.49 = f32[32,128,256]{2,0,1:T(8,128)S(1)} fusion(f32[80,128,256]{2,0,1:T(8,128)} %copy.42, s32[80]{0:T(128)S(1)} %bitcast.82), kind=kOutput, calls=%fused_computation.39 | convolution fusion | flops 1006635520 | bytes 14680384 | tf_op jit(solution)/shard_map/rt,taf->raf/dot_general | solution.py:26
  174.0 78.6 %reduce-scatter.5.cloned.1.call-done = f32[256,256]{1,0:T(8,128)} async-done(((f32[4096,256]{1,0:T(8,128)}), f32[256,256]{1,0:T(8,128)}) %reduce-scatter.5.cloned.1.call-update) | async-done | bytes 262160 | tf_op jit(solution)/shard_map/reduce_scatter | solution.py:67
  256.9 48.8 %all-gather.11.cloned.1.call-done = f32[4096,256]{1,0:T(8,128)} async-done(((f32[256,256]{1,0:T(8,128)}), f32[4096,256]{1,0:T(8,128)}) %all-gather.11.cloned.1.call-update) | async-done | bytes 4194320 | tf_op jit(solution)/shard_map/all_gather | solution.py:80
  305.8 10.0 %gather_fusion.3 = f32[80,128,256]{2,1,0:T(8,128)} fusion(f32[32,128,256]{2,1,0:T(8,128)} %bitcast.73, s32[1024]{0:T(1024)S(1)} %pad_clamp_fusion), kind=kCustom, calls=%fused_computation.3.clone | custom fusion | bytes 20971840 | tf_op jit(solution)/shard_map/jit(_take)/gather | solution.py:34
  315.8 23.3 %fusion.35 = f32[80,128,256]{1,2,0:T(8,128)} fusion(f32[1,1,80,128,128]{4,3,2,1,0:T(8,128)} %param.14, f32[80,128,256]{2,1,0:T(8,128)} %gather_fusion.3, pred[80]{0:T(512)(128)(4,1)S(1)} %get-tuple-element.24), kind=kOutput, calls=%fused_computation.27 | convolution fusion | flops 4029153280 | bytes 26214480 | tf_op jit(solution)/shard_map/tba,tbf->taf/dot_general | solution.py:35
  339.0 11.7 %copy.51 = f32[80,128,256]{2,0,1:T(8,128)} copy(f32[80,128,256]{1,2,0:T(8,128)} %fusion.35) | data formatting | bytes 20971520 | tf_op jit(solution)/shard_map/tba,tbf->taf/dot_general | solution.py:35
  350.7 6.3 fusion.55
  361.1 9.7 %gather_fusion.1 = f32[80,128,256]{2,1,0:T(8,128)} fusion(f32[16,128,256]{2,1,0:T(8,128)} %bitcast.71, s32[1024]{0:T(1024)S(1)} %pad_clamp_fusion.1), kind=kCustom, calls=%fused_computation.2.clone | custom fusion | bytes 20971840 | tf_op jit(solution)/shard_map/jit(_take)/gather | solution.py:21
  370.8 22.5 %reduce-scatter.11.cloned.1.call-done = f32[256,256]{1,0:T(8,128)} async-done(((f32[2048,256]{1,0:T(8,128)}), f32[256,256]{1,0:T(8,128)}) %reduce-scatter.11.cloned.1.call-update) | async-done | bytes 262160 | tf_op jit(solution)/shard_map/reduce_scatter | solution.py:82
  395.6 23.1 %fusion.25 = f32[80,128,256]{1,2,0:T(8,128)} fusion(f32[1,1,80,128,128]{4,3,2,1,0:T(8,128)} %param.14, f32[80,128,256]{2,1,0:T(8,128)} %gather_fusion.1, pred[80]{0:T(512)(128)(4,1)S(1)} %compare_and_fusion.1), kind=kOutput, calls=%fused_computation.25 | convolution fusion | flops 4029153280 | bytes 26214480 | tf_op jit(solution)/shard_map/tab,tbf->taf/dot_general | solution.py:22
  418.7 11.7 %copy.45 = f32[80,128,256]{2,0,1:T(8,128)} copy(f32[80,128,256]{1,2,0:T(8,128)} %fusion.25) | data formatting | bytes 20971520 | tf_op jit(solution)/shard_map/tab,tbf->taf/dot_general | solution.py:22
  430.3 50.7 %all-reduce.5.cloned.1.call-done = (f32[128,256]{0,1:T(8,128)}, f32[256,256]{1,0:T(8,128)}) async-done(((f32[128,256]{0,1:T(8,128)}, f32[256,256]{1,0:T(8,128)}), (f32[128,256]{0,1:T(8,128)}, f32[256,256]{1,0:T(8,128)})) %all-reduce.5.cloned.1.call-update) | async-done | bytes 393232 | tf_op jit(solution)/shard_map/psum | solution.py:11
  481.3 6.9 %fusion.47 = f32[32,128,256]{2,0,1:T(8,128)S(1)} fusion(f32[80,128,256]{2,0,1:T(8,128)} %copy.45, s32[80]{0:T(128)S(1)} %bitcast.83), kind=kOutput, calls=%fused_computation.38 | convolution fusion | flops 1006635520 | bytes 14680384 | tf_op jit(solution)/shard_map/rt,taf->raf/dot_general | solution.py:26
  492.6 50.8 %all-reduce.7.cloned.1.call-done = (f32[128,256]{0,1:T(8,128)}, f32[256,256]{1,0:T(8,128)}) async-done(((f32[128,256]{0,1:T(8,128)}, f32[256,256]{1,0:T(8,128)}), (f32[128,256]{0,1:T(8,128)}, f32[256,256]{1,0:T(8,128)})) %all-reduce.7.cloned.1.call-update) | async-done | bytes 393232 | tf_op jit(solution)/shard_map/psum | solution.py:12
  545.1 80.2 %reduce-scatter.7.cloned.1.call-done = f32[256,256]{1,0:T(8,128)} async-done(((f32[4096,256]{1,0:T(8,128)}), f32[256,256]{1,0:T(8,128)}) %reduce-scatter.7.cloned.1.call-update) | async-done | bytes 262160 | tf_op jit(solution)/shard_map/reduce_scatter | solution.py:72
  (52 shorter events, 30.8 us)
Async XLA Ops:
  7.2 245.4 %copy-start = (f32[256,256]{1,0:T(8,128)S(1)}, f32[256,256]{1,0:T(8,128)}, u32[]{:S(2)}) copy-start(f32[256,256]{1,0:T(8,128)} %param.16) | copy-start | bytes 786436
  7.2 57.0 %all-gather.9.cloned.1.call-start = ((), (), s32[]{:S(2)}) async-start(), calls=%async_computation.9 | async-start | bytes 4456448 | tf_op jit(solution)/shard_map/all_gather | solution.py:73
  7.9 110.1 %all-gather.5.cloned.1.call-start = ((), (), s32[]{:S(2)}) async-start(), calls=%async_computation.5 | async-start | bytes 2359296 | tf_op jit(solution)/shard_map/all_gather | solution.py:65
  21.2 152.7 %reduce-scatter.9.cloned.1.call-start = ((), (), s32[]{:S(2)}) async-start(), calls=%async_computation.10 | async-start | bytes 2359296 | tf_op jit(solution)/shard_map/reduce_scatter | solution.py:75
  97.1 11.7 %copy-start.3 = (s32[1,1,80]{2,1,0:T(1,128)S(1)}, s32[1,1,80]{2,1,0:T(1,128)}, u32[]{:S(2)}) copy-start(s32[1,1,80]{2,1,0:T(1,128)} %param.13) | copy-start | bytes 964
  117.6 135.0 %reduce-scatter.5.cloned.1.call-start = ((), (), s32[]{:S(2)}) async-start(), calls=%async_computation.6 | async-start | bytes 4456448 | tf_op jit(solution)/shard_map/reduce_scatter | solution.py:67
  150.9 11.6 %copy-start.2 = (s32[1,1,80]{2,1,0:T(1,128)S(1)}, s32[1,1,80]{2,1,0:T(1,128)}, u32[]{:S(2)}) copy-start(s32[1,1,80]{2,1,0:T(1,128)} %param.12) | copy-start | bytes 964
  173.9 131.8 %all-gather.11.cloned.1.call-start = ((), (), s32[]{:S(2)}) async-start(), calls=%async_computation.11 | async-start | bytes 4456448 | tf_op jit(solution)/shard_map/all_gather | solution.py:80
  254.7 106.4 %all-gather.7.cloned.1.call-start = ((), (), s32[]{:S(2)}) async-start(), calls=%async_computation.7 | async-start | bytes 2359296 | tf_op jit(solution)/shard_map/all_gather | solution.py:70
  256.9 136.4 %reduce-scatter.11.cloned.1.call-start = ((), (), s32[]{:S(2)}) async-start(), calls=%async_computation.12 | async-start | bytes 2359296 | tf_op jit(solution)/shard_map/reduce_scatter | solution.py:82
  350.7 9.1 %copy-start.4 = (f32[256,256]{1,0:T(8,128)S(1)}, f32[256,256]{1,0:T(8,128)}, u32[]{:S(2)}) copy-start(f32[256,256]{1,0:T(8,128)} %reduce-scatter.9.cloned.1.call-done) | copy-start | bytes 786436
  350.7 9.1 %copy-start.5 = (f32[256,256]{1,0:T(8,128)S(1)}, f32[256,256]{1,0:T(8,128)}, u32[]{:S(2)}) copy-start(f32[256,256]{1,0:T(8,128)} %reduce-scatter.5.cloned.1.call-done) | copy-start | bytes 786436
  359.5 121.5 %all-reduce.5.cloned.1.call-start = ((), (), s32[]{:S(2)}) async-start(), calls=%async_computation.13 | async-start | bytes 786432 | tf_op jit(solution)/shard_map/psum | solution.py:11
  395.5 147.9 %all-reduce.7.cloned.1.call-start = ((), (), s32[]{:S(2)}) async-start(), calls=%async_computation.14 | async-start | bytes 786432 | tf_op jit(solution)/shard_map/psum | solution.py:12
  481.0 145.9 %copy-start.1 = (f32[256,256]{1,0:T(8,128)S(1)}, f32[256,256]{1,0:T(8,128)}, u32[]{:S(2)}) copy-start(f32[256,256]{1,0:T(8,128)} %param.16) | copy-start | bytes 786436
  481.0 144.3 %reduce-scatter.7.cloned.1.call-start = ((), (), s32[]{:S(2)}) async-start(), calls=%async_computation.8 | async-start | bytes 4456448 | tf_op jit(solution)/shard_map/reduce_scatter | solution.py:72
Sparse Core Ops, SparseCore 0:
  10.1 53.9 all-gather.8
  66.5 24.8 all-gather.4
  117.7 33.6 reduce-scatter.8
  174.0 78.4 reduce-scatter.4
  255.1 50.5 all-gather.10
  307.9 24.8 all-gather.6
  359.6 33.6 reduce-scatter.10
  397.2 83.7 all-reduce.4
  483.4 59.9 all-reduce.6
  547.2 78.0 reduce-scatter.6
